TPU v7x, 128 devices: a whole 4x4x4 slice. The times are simulated.
128 devices in a mesh: vir: 8 (over y_hi, x), occ: 16 (over y_lo, z, core).
Axes of the slice: x: 4, y: 4 (y_hi: 2, y_lo: 2; y = y_hi * 2 + y_lo), z: 4, core: 2. Of those that a mesh axis runs over, the one named last changes fastest.
Arguments:
- amplitudes: bfloat16 [4096, 8192], P('occ', 'vir'), may hold values from -6 to 6
- ladder_integrals: bfloat16 [8192, 8192], P('occ', 'vir'), may hold values from -0.0625 to 0.0625
- crossed_integrals: bfloat16 [2, 4096, 4096], P(None, 'occ', 'vir'), may hold values from -0.09375 to 0.09375
- vir_counts: int32 [8], replicated, may hold values from 1 to 64, 480 in all
Outputs:
- residual: bfloat16 [4096, 8192], P('occ', 'vir')
Inputs may be any that keep to these rules, and one draw needn't show every extreme that they name: `vir_counts`: the counts of all 8 irreps sum to 480 and the largest is exactly 64.
All inputs are finite; a program needn't handle non-finite values.
Results may differ from a plain program's by a relative error of at most 0.004.
Values may be sent and summed in bfloat16 or wider, within the bound.
A program may use at most 128 MiB of HBM per device.

v0:
```python
import jax
import jax.numpy as jnp
from jax import lax
from jax.sharding import PartitionSpec as P

O = 64
VS = 64
NB = 2
BP = 4096


def build_mask(vir_counts):
    slot_index = jnp.arange(VS, dtype=jnp.int32)
    blocks = []
    for block_index in range(NB):
        first_act = (slot_index < vir_counts[2 * block_index]).astype(jnp.float32)
        second_act = (slot_index < vir_counts[2 * block_index + 1]).astype(jnp.float32)
        blocks.append((first_act[:, None] * second_act[None, :]).reshape(BP))
    return jnp.concatenate(blocks)


def per_device(amplitudes, ladder_integrals, crossed_integrals, vir_counts):
    local_rows = amplitudes.shape[0]
    col_width = amplitudes.shape[1]
    full_mask = build_mask(vir_counts)
    column_mask = lax.dynamic_slice_in_dim(full_mask, lax.axis_index("vir") * col_width, col_width)
    masked = amplitudes * column_mask.astype(jnp.bfloat16)[None, :]
    spread = lax.all_gather(masked, "vir", axis=1, tiled=True)
    regrouped = lax.all_to_all(spread, "occ", split_axis=1, concat_axis=0, tiled=True)
    ladder = lax.psum_scatter(
        jnp.dot(regrouped, ladder_integrals, preferred_element_type=jnp.float32),
        "occ",
        scatter_dimension=0,
        tiled=True,
    )
    occ_local = local_rows // O
    reordered = (
        spread.reshape(occ_local, O, NB, VS, VS)
        .transpose(2, 0, 3, 1, 4)
        .reshape(NB, occ_local * VS, O * VS)
    )
    crossed_cols = crossed_integrals.shape[2]
    crossed_sum = jnp.einsum(
        "gxy,gyz->gxz",
        reordered,
        lax.all_gather(crossed_integrals, "occ", axis=1, tiled=True),
        preferred_element_type=jnp.float32,
    )
    crossed_term = crossed_sum.astype(jnp.bfloat16)
    occ_cols = crossed_cols // VS
    arranged = (
        crossed_term.reshape(NB, occ_local, VS, occ_cols, VS)
        .transpose(1, 3, 0, 2, 4)
        .reshape(occ_local, occ_cols, NB * VS, VS)
    )
    returned = lax.all_to_all(arranged, "vir", split_axis=2, concat_axis=1, tiled=True)
    returned = returned.reshape(local_rows, col_width)
    total = (ladder + returned.astype(jnp.float32)) * column_mask[None, :]
    return total.astype(jnp.bfloat16)


def solution(mesh):
    in_specs = (P("occ", "vir"), P("occ", "vir"), P(None, "occ", "vir"), P())
    out_specs = P("occ", "vir")
    return jax.shard_map(
        per_device, mesh=mesh, in_specs=in_specs, out_specs=out_specs, check_vma=False
    )
```

profile of v0, /device:TPU:0, one launch (start us, length us, event | category | flops | bytes accessed | tf_op | source)
XLA Modules:
  0.0 294.8 jit_solution(6605446424760793672)
XLA Ops:
  6.5 0.0 copy-start
  6.5 0.0 all-gather.3.cloned.1.call-start
  6.5 1.4 fusion.3
  8.0 1.3 compare_convert_fusion.2
  9.3 0.1 broadcast_multiply_fusion.2
  9.3 0.1 mul.56
  9.4 1.2 compare_convert_fusion
  10.6 0.1 broadcast_multiply_fusion.1
  10.7 0.1 mul.60
  10.8 1.2 copy.16
  12.0 1.0 broadcast_multiply_fusion
  13.0 0.0 all-gather.3.cloned.1.call-update
  13.1 0.0 all-gather.5.cloned.1.call-start
  13.1 0.7 all-gather.5.cloned.1.call-update
  13.8 0.0 reduce-scatter.2.cloned.1.call-start
  13.9 73.4 %all-gather.3.cloned.1.call-done = bf16[256,8192]{0,1:T(8,128)(2,1)} async-done(((bf16[256,1024]{0,1:T(8,128)(2,1)}), bf16[256,8192]{0,1:T(8,128)(2,1)}) %all-gather.3.cloned.1.call-update) | async-done | bytes 4194320 | tf_op jit(solution)/shard_map/all_gather | solution.py:28
  87.2 82.5 %all_to_all.28 = bf16[256,16,512]{0,2,1:T(8,128)(2,1)} all-to-all(bf16[256,16,512]{0,2,1:T(8,128)(2,1)} %bitcast.27), channel_id=1, replica_groups=mesh['vir'=8,'occ'=16] {'occ'}, dimensions={1} | all-to-all | bytes 8388608 | tf_op jit(solution)/shard_map/all_to_all | solution.py:29
  169.7 6.5 %copy.17 = bf16[16,256,512]{2,1,0:T(8,128)(2,1)} copy(bf16[16,256,512]{1,2,0:T(8,128)(2,1)} %bitcast.28) | data formatting | bytes 8388608 | tf_op jit(solution)/shard_map/all_to_all | solution.py:29
  176.2 0.0 copy-done
  176.2 10.3 %fusion.4 = f32[4096,1024]{1,0:T(8,128)} fusion(bf16[4096,512]{1,0:T(8,128)(2,1)} %bitcast.30, bf16[512,1024]{1,0:T(8,128)(2,1)S(1)} %copy-done), kind=kOutput, calls=%fused_computation.15 | convolution fusion | flops 4294967296 | bytes 22020096 | tf_op jit(solution)/shard_map/dot_general | solution.py:31
  186.5 0.0 reduce-scatter.2.cloned.1.call-update
  186.5 12.9 %reshape.51 = bf16[4,64,2,64,64]{1,0,4,3,2:T(4,128)(2,1)} reshape(bf16[256,8192]{0,1:T(8,128)(2,1)} %all-gather.3.cloned.1.call-done) | data formatting | bytes 8388608 | tf_op jit(solution)/shard_map/reshape | solution.py:38
  199.5 13.8 %copy.18 = bf16[4,64,2,64,64]{4,1,3,0,2:T(8,128)(2,1)} copy(bf16[4,64,2,64,64]{1,0,4,3,2:T(4,128)(2,1)} %reshape.51) | data formatting | bytes 8388608 | tf_op jit(solution)/shard_map/reshape | solution.py:38
  213.3 12.1 %reshape.52 = bf16[2,256,4096]{2,1,0:T(8,128)(2,1)} reshape(bf16[2,4,64,64,64]{4,3,2,1,0:T(8,128)(2,1)} %bitcast.26) | data formatting | bytes 8388608 | tf_op jit(solution)/shard_map/reshape | solution.py:40
  225.4 0.0 all-gather.5.cloned.1.call-done
  225.4 7.2 %convolution_convert_fusion = bf16[2,256,512]{2,1,0:T(8,128)(2,1)S(1)} fusion(bf16[2,256,4096]{2,1,0:T(8,128)(2,1)} %reshape.52, bf16[2,4096,512]{2,1,0:T(8,128)(2,1)} %all-gather.5.cloned.1.call-done), kind=kOutput, calls=%fused_computation.1 | convolution fusion | flops 2147745792 | bytes 13107200 | tf_op jit(solution)/shard_map/gxy,gyz->gxz/dot_general | solution.py:43
  232.6 0.5 reshape.53
  233.1 1.0 copy.19
  234.1 1.1 copy.23
  235.2 0.7 reshape.57
  236.0 13.1 %all_to_all.29 = bf16[8,2,16384]{2,1,0:T(2,128)(2,1)S(1)} all-to-all(bf16[8,2,16384]{2,1,0:T(2,128)(2,1)S(1)} %reshape.57), channel_id=1, replica_groups=mesh['vir'=8,'occ'=16] {'vir'}, dimensions={0} | all-to-all | bytes 1048576 | tf_op jit(solution)/shard_map/all_to_all | solution.py:56
  249.0 0.7 reshape.58
  249.7 0.4 copy.21
  250.1 0.0 copy-start.1
  250.1 0.3 convert_bitcast_fusion
  250.4 0.2 copy.22
  250.6 1.5 reshape.55
  252.2 33.6 %reduce-scatter.2.cloned.1.call-done = f32[256,1024]{1,0:T(8,128)} async-done(((f32[4096,1024]{1,0:T(8,128)}), f32[256,1024]{1,0:T(8,128)}) %reduce-scatter.2.cloned.1.call-update) | async-done | bytes 1048592 | tf_op jit(solution)/shard_map/reduce_scatter | solution.py:30
  285.7 2.5 multiply_convert_fusion
  288.3 0.0 copy-done.1
  (1 shorter events, 0.0 us)
Async XLA Ops:
  6.5 169.6 %copy-start = (bf16[512,1024]{1,0:T(8,128)(2,1)S(1)}, bf16[512,1024]{1,0:T(8,128)(2,1)}, u32[]{:S(2)}) copy-start(bf16[512,1024]{1,0:T(8,128)(2,1)} %param.5) | copy-start | bytes 3145732
  6.5 80.7 %all-gather.3.cloned.1.call-start = ((), (), s32[]{:S(2)}) async-start(), calls=%async_computation.3 | async-start | bytes 4718592 | tf_op jit(solution)/shard_map/all_gather | solution.py:28
  13.1 212.3 %all-gather.5.cloned.1.call-start = ((), (), s32[]{:S(2)}) async-start(), calls=%async_computation.5 | async-start | bytes 8912896 | tf_op jit(solution)/shard_map/all_gather | solution.py:46
  13.8 271.9 %reduce-scatter.2.cloned.1.call-start = ((), (), s32[]{:S(2)}) async-start(), calls=%async_computation.4 | async-start | bytes 17825792 | tf_op jit(solution)/shard_map/reduce_scatter | solution.py:30
  250.1 38.2 %copy-start.1 = (bf16[512,1024]{1,0:T(8,128)(2,1)S(1)}, bf16[512,1024]{1,0:T(8,128)(2,1)}, u32[]{:S(2)}) copy-start(bf16[512,1024]{1,0:T(8,128)(2,1)} %param.5) | copy-start | bytes 3145732
Sparse Core Ops, SparseCore 0:
  13.2 74.0 all-gather.2
  88.9 91.8 all-gather.4
  186.7 99.0 reduce-scatter.1
where the time goes:
time: 296 us; the launch traced here: 295 us
  waiting for transfers between devices  108 us (36%)
  blocking collectives  95.5 us (32%)
  local copies, waits for them, and re-layouts  54.3 us (18%)
  matrix products  17.5 us (6%)
  between operations  13.2 us (4%)
  other arithmetic  6.43 us (2%)
    all_to_all x1, blocking collectives, per_device(): lax.all_to_all(spread, 'occ', split_axis=1, concat_axis=0, tiled=True)  82.5 us
    all_gather x1, waiting for transfers between devices, per_device(): spread = lax.all_gather(masked, 'vir', axis=1, tiled=True)  73.4 us
    reduce_scatter x1, waiting for transfers between devices, per_device(): lax.psum_scatter(jnp.dot(regrouped, ladder_integrals, preferred_element_t...  33.6 us
    reshape x2, local copies, waits for them, and re-layouts, per_device(): spread.reshape(occ_local, O, NB, VS, VS).transpose(2, 0, 3, 1, 4)  26.7 us
    all_to_all x1, blocking collectives, per_device(): lax.all_to_all(arranged, 'vir', split_axis=2, concat_axis=1, tiled=True)  13.1 us
    reshape x1, local copies, waits for them, and re-layouts, per_device(): reordered = spread.reshape(occ_local, O, NB, VS, VS).transpose(2, 0, 3, 1...  12.1 us
    dot_general x1, matrix products, per_device(): jnp.dot(regrouped, ladder_integrals, preferred_element_type=jnp.float32)  10.3 us
    dot_general x1, matrix products, per_device(): jnp.einsum('gxy,gyz->gxz', reordered, lax.all_gather(crossed_integrals, '...  7.19 us
  transfers between devices with their start and end apart: 3, of which 2 were waited for; matrix products, arithmetic and copies ran while one was open for 24% of the time, Pallas kernels for 0%

commit v1 on v0

--- a/solution.py
+++ b/solution.py
@@ -25,7 +25,9 @@
     full_mask = build_mask(vir_counts)
     column_mask = lax.dynamic_slice_in_dim(full_mask, lax.axis_index("vir") * col_width, col_width)
     masked = amplitudes * column_mask.astype(jnp.bfloat16)[None, :]
-    spread = lax.all_gather(masked, "vir", axis=1, tiled=True)
+    spread = jnp.concatenate(
+        lax.all_to_all(jnp.stack([masked] * lax.axis_size("vir")), "vir", 0, 0), axis=1
+    )
     regrouped = lax.all_to_all(spread, "occ", split_axis=1, concat_axis=0, tiled=True)
     ladder = lax.psum_scatter(
         jnp.dot(regrouped, ladder_integrals, preferred_element_type=jnp.float32),

time: 296 us -> 284 us (0.959)
  waiting for transfers between devices: 108 us -> 28.9 us
  blocking collectives: 95.5 us -> 159 us
  local copies, waits for them, and re-layouts: 54.3 us -> 57.5 us
    all_gather x1 -> x0, waiting for transfers between devices: 73.4 us -> none  [per_device(): spread = lax.all_gather(masked, 'vir', axis=1, tiled=True)]
    all_to_all x0 -> x1, blocking collectives: none -> 67.6 us  [per_device(): lax.all_to_all(jnp.stack([masked] * lax.axis_size('vir')), 'vir', 0, 0)]
    reshape x2 -> x1, local copies, waits for them, and re-layouts: 26.7 us -> 6.79 us  [per_device(): jnp.concatenate(lax.all_to_all(jnp.stack([masked] * lax.axis_size('vir'))...]
    transpose x0 -> x1, local copies, waits for them, and re-layouts: none -> 12.2 us  [per_device(): reordered = spread.reshape(occ_local, O, NB, VS, VS).transpose(2, 0, 3, 1...]
    another operation x0 -> x2, local copies, waits for them, and re-layouts: none -> 12 us  [the longest x1 11.8 us: per_device(): spread.reshape(occ_local, O, NB, VS, VS).transpose(2, 0, 3, 1, 4)]
    all_to_all x1, blocking collectives: 82.5 us -> 73.7 us  [per_device(): lax.all_to_all(spread, 'occ', split_axis=1, concat_axis=0, tiled=True)]
    reduce_scatter x1, waiting for transfers between devices: 33.6 us -> 28.2 us  [per_device(): lax.psum_scatter(jnp.dot(regrouped, ladder_integrals, preferred_element_t...]
    all_to_all x1, blocking collectives: 13.1 us -> 17.9 us  [per_device(): lax.all_to_all(arranged, 'vir', split_axis=2, concat_axis=1, tiled=True)]
  transfers between devices with their start and end apart: 3 -> 2, of which waited for: 2 -> 1; matrix products, arithmetic and copies ran while one was open for 24% -> 28% of each run, Pallas kernels for 0% -> 0%
where the time goes in v1:
time: 284 us; the launch traced here: 283 us
  blocking collectives  159 us (56%)
  local copies, waits for them, and re-layouts  57.5 us (20%)
  waiting for transfers between devices  28.9 us (10%)
  matrix products  17.5 us (6%)
  between operations  13.5 us (5%)
  other arithmetic  6.57 us (2%)
    all_to_all x1, blocking collectives, per_device(): lax.all_to_all(spread, 'occ', split_axis=1, concat_axis=0, tiled=True)  73.7 us
    all_to_all x1, blocking collectives, per_device(): lax.all_to_all(jnp.stack([masked] * lax.axis_size('vir')), 'vir', 0, 0)  67.6 us
    reduce_scatter x1, waiting for transfers between devices, per_device(): lax.psum_scatter(jnp.dot(regrouped, ladder_integrals, preferred_element_t...  28.2 us
    all_to_all x1, blocking collectives, per_device(): lax.all_to_all(arranged, 'vir', split_axis=2, concat_axis=1, tiled=True)  17.9 us
    transpose x1, local copies, waits for them, and re-layouts, per_device(): reordered = spread.reshape(occ_local, O, NB, VS, VS).transpose(2, 0, 3, 1...  12.2 us
    reshape x1, local copies, waits for them, and re-layouts, per_device(): reordered = spread.reshape(occ_local, O, NB, VS, VS).transpose(2, 0, 3, 1...  12.2 us
    another operation x1, local copies, waits for them, and re-layouts, per_device(): spread.reshape(occ_local, O, NB, VS, VS).transpose(2, 0, 3, 1, 4)  11.8 us
    dot_general x1, matrix products, per_device(): jnp.dot(regrouped, ladder_integrals, preferred_element_type=jnp.float32)  10.3 us
  transfers between devices with their start and end apart: 2, of which 1 were waited for; matrix products, arithmetic and copies ran while one was open for 28% of the time, Pallas kernels for 0%

profile of v1, /device:TPU:0, one launch (start us, length us, event | category | flops | bytes accessed | tf_op | source)
XLA Modules:
  0.0 283.3 jit_solution(10641433144881022020)
XLA Ops:
  6.5 0.0 copy-start
  6.5 0.0 all-gather.2.cloned.1.call-start
  6.5 0.7 all-gather.2.cloned.1.call-update
  7.3 0.0 reduce-scatter.2.cloned.1.call-start
  7.3 1.5 fusion.3
  8.8 1.3 compare_convert_fusion.2
  10.1 0.1 broadcast_multiply_fusion.2
  10.1 0.1 mul.56
  10.2 1.3 compare_convert_fusion
  11.5 0.1 broadcast_multiply_fusion.1
  11.6 0.1 mul.60
  11.6 1.1 broadcast_multiply_fusion
  12.7 0.2 copy.12
  12.9 0.3 stack.2
  13.2 67.6 %all_to_all.33 = bf16[8,256,1024]{1,2,0:T(8,128)(2,1)S(1)} all-to-all(bf16[8,256,1024]{1,2,0:T(8,128)(2,1)S(1)} %stack.2), channel_id=1, replica_groups=mesh['vir'=8,'occ'=16] {'vir'}, dimensions={0} | all-to-all | bytes 8388608 | tf_op jit(solution)/shard_map/all_to_all | solution.py:29
  80.8 0.0 copy-start.2
  80.8 73.7 %all_to_all.34 = bf16[256,16,512]{0,2,1:T(8,128)(2,1)} all-to-all(bf16[256,16,512]{0,2,1:T(8,128)(2,1)S(1)} %bitcast.26), channel_id=1, replica_groups=mesh['vir'=8,'occ'=16] {'occ'}, dimensions={1} | all-to-all | bytes 8388608 | tf_op jit(solution)/shard_map/all_to_all | solution.py:31
  154.5 0.0 copy-done.2
  154.5 6.4 %copy.13 = bf16[16,256,512]{2,1,0:T(8,128)(2,1)} copy(bf16[16,256,512]{1,2,0:T(8,128)(2,1)} %bitcast.29) | data formatting | bytes 8388608 | tf_op jit(solution)/shard_map/all_to_all | solution.py:31
  160.9 0.0 copy-done
  160.9 10.3 %fusion.4 = f32[4096,1024]{1,0:T(8,128)} fusion(bf16[4096,512]{1,0:T(8,128)(2,1)} %bitcast.31, bf16[512,1024]{1,0:T(8,128)(2,1)S(1)} %copy-done), kind=kOutput, calls=%fused_computation.15 | convolution fusion | flops 4294967296 | bytes 22020096 | tf_op jit(solution)/shard_map/dot_general | solution.py:33
  171.2 0.0 reduce-scatter.2.cloned.1.call-update
  171.2 6.8 %copy.14 = bf16[256,8,1024]{2,1,0:T(8,128)(2,1)} copy(bf16[256,8,1024]{0,2,1:T(8,128)(2,1)} %bitcast.27) | data formatting | bytes 8388608 | tf_op jit(solution)/shard_map/reshape | solution.py:28
  178.0 11.8 %reshape_reshape.3 = bf16[4,64,2,64,64]{4,3,2,1,0:T(8,128)(2,1)} reshape(bf16[256,8,1024]{2,1,0:T(8,128)(2,1)} %copy.14) | data formatting | bytes 8388608 | tf_op jit(solution)/shard_map/reshape;reshape | solution.py:40
  189.7 12.2 %copy.15 = bf16[2,4,64,64,64]{4,3,2,1,0:T(8,128)(2,1)} copy(bf16[2,4,64,64,64]{4,2,0,3,1:T(8,128)(2,1)} %bitcast.28) | data formatting | bytes 8388608 | tf_op jit(solution)/shard_map/transpose | solution.py:41
  201.9 12.2 %reshape.56 = bf16[2,256,4096]{2,1,0:T(8,128)(2,1)} reshape(bf16[2,4,64,64,64]{4,3,2,1,0:T(8,128)(2,1)} %copy.15) | data formatting | bytes 8388608 | tf_op jit(solution)/shard_map/reshape | solution.py:42
  214.0 0.0 all-gather.2.cloned.1.call-done
  214.0 7.2 %convolution_convert_fusion = bf16[2,256,512]{2,1,0:T(8,128)(2,1)S(1)} fusion(bf16[2,256,4096]{2,1,0:T(8,128)(2,1)} %reshape.56, bf16[2,4096,512]{2,1,0:T(8,128)(2,1)} %all-gather.2.cloned.1.call-done), kind=kOutput, calls=%fused_computation.1 | convolution fusion | flops 2147745792 | bytes 13107200 | tf_op jit(solution)/shard_map/gxy,gyz->gxz/dot_general | solution.py:45
  221.3 0.5 reshape.57
  221.8 1.0 copy.16
  222.8 1.1 copy.20
  223.9 0.7 reshape.61
  224.6 17.9 %all_to_all.35 = bf16[8,2,16384]{2,1,0:T(2,128)(2,1)S(1)} all-to-all(bf16[8,2,16384]{2,1,0:T(2,128)(2,1)S(1)} %reshape.61), channel_id=1, replica_groups=mesh['vir'=8,'occ'=16] {'vir'}, dimensions={0} | all-to-all | bytes 1048576 | tf_op jit(solution)/shard_map/all_to_all | solution.py:58
  242.6 0.7 reshape.62
  243.2 0.4 copy.18
  243.6 0.0 copy-start.1
  243.6 0.3 convert_bitcast_fusion
  243.9 0.2 copy.19
  244.1 1.6 reshape.59
  245.7 28.2 %reduce-scatter.2.cloned.1.call-done = f32[256,1024]{1,0:T(8,128)} async-done(((f32[4096,1024]{1,0:T(8,128)}), f32[256,1024]{1,0:T(8,128)}) %reduce-scatter.2.cloned.1.call-update) | async-done | bytes 1048592 | tf_op jit(solution)/shard_map/reduce_scatter | solution.py:32
  273.9 2.5 multiply_convert_fusion
  276.4 0.0 copy-done.1
  (1 shorter events, 0.0 us)
Async XLA Ops:
  6.5 154.3 %copy-start = (bf16[512,1024]{1,0:T(8,128)(2,1)S(1)}, bf16[512,1024]{1,0:T(8,128)(2,1)}, u32[]{:S(2)}) copy-start(bf16[512,1024]{1,0:T(8,128)(2,1)} %param.5) | copy-start | bytes 3145732
  6.5 207.5 %all-gather.2.cloned.1.call-start = ((), (), s32[]{:S(2)}) async-start(), calls=%async_computation.5 | async-start | bytes 8912896 | tf_op jit(solution)/shard_map/all_gather | solution.py:48
  7.3 266.7 %reduce-scatter.2.cloned.1.call-start = ((), (), s32[]{:S(2)}) async-start(), calls=%async_computation.4 | async-start | bytes 17825792 | tf_op jit(solution)/shard_map/reduce_scatter | solution.py:32
  80.8 73.7 %copy-start.2 = (bf16[8,256,1024]{1,2,0:T(8,128)(2,1)}, bf16[8,256,1024]{1,2,0:T(8,128)(2,1)S(1)}, u32[]{:S(2)}) copy-start(bf16[8,256,1024]{1,2,0:T(8,128)(2,1)S(1)} %all_to_all.33) | copy-start | bytes 12582916
  243.6 32.8 %copy-start.1 = (bf16[512,1024]{1,0:T(8,128)(2,1)S(1)}, bf16[512,1024]{1,0:T(8,128)(2,1)}, u32[]{:S(2)}) copy-start(bf16[512,1024]{1,0:T(8,128)(2,1)} %param.5) | copy-start | bytes 3145732
Sparse Core Ops, SparseCore 0:
  9.0 130.9 all-gather.1
  171.3 102.5 reduce-scatter.1
